TPU v7x, 256 devices: a whole 4x4x8 slice. The times are simulated.
256 devices in a mesh: grp: 4 (over x), ep: 64 (over y, z, core).
Axes of the slice: x: 4, y: 4, z: 8, core: 2. Of those that a mesh axis runs over, the one named last changes fastest.
Arguments:
- queries: bfloat16 [6144, 4096], P(('grp', 'ep')), may hold values from -9 to 9
- new_keys: bfloat16 [6144, 512], P(('grp', 'ep')), may hold values from -9 to 9
- new_values: bfloat16 [6144, 512], P(('grp', 'ep')), may hold values from -6 to 6
- key_cache: bfloat16 [4096, 48, 512], P(('grp', 'ep')), may hold values from -9 to 9
- value_cache: bfloat16 [4096, 48, 512], P(('grp', 'ep')), may hold values from -6 to 6
- cache_len: int32 [4096], P(('grp', 'ep')), may hold values from 2 to 48, as said below
- residual: bfloat16 [6144, 2048], P(('grp', 'ep')), may hold values from -17 to 17
- out_proj: bfloat16 [4096, 2048], P(None, 'grp'), may hold values from -0.09375 to 0.09375
- norm_gain: float32 [2048], P('grp'), may hold values from 0.1 to 1.9
- expert_ids: int32 [6144, 8], P(('grp', 'ep')), may hold values from 0 to 127, as said below
- route_weights: bfloat16 [6144, 8], P(('grp', 'ep')), may hold values from 0.049804688 to 1
- slot_expert: int32 [192], replicated, may hold values from 0 to 127, as said below
- gate_up: bfloat16 [192, 2048, 1536], P('ep', 'grp'), may hold values from -1 to 1, as said below
- down_proj: bfloat16 [192, 768, 2048], P('ep', None, 'grp'), may hold values from -2 to 2, as said below
Outputs:
- moe_out: bfloat16 [6144, 2048], P(('grp', 'ep'))
- layer_out: bfloat16 [6144, 2048], P(('grp', 'ep'))
Inputs may be any that keep to these rules, and one draw needn't show every extreme that they name: `expert_ids`: each row names 8 different experts. In the rows of one device one expert, the same on all devices, is named by exactly 3 rows, and every other expert by at most 2 rows; some expert other than it is named by exactly 2 rows of a device. `slot_expert`: every expert is held by one or two slots; the expert named by 3 rows of every device is held by two. `cache_len`: some request has exactly 48 cached tokens. `gate_up`: slots holding the same expert hold equal weights. `down_proj`: slots holding the same expert hold equal weights.
All inputs are finite; a program needn't handle non-finite values.
Results may differ from a plain program's by a relative error of at most 0.033.
Values may be sent and summed in bfloat16 or wider, within the bound.
A program may use at most 128 MiB of HBM per device.

v0:
```python
import math
import jax
import jax.numpy as jnp
from jax import lax
from jax.sharding import PartitionSpec as P

D = 2048
HEADS = 32
KV_HEADS = 4
HEAD_DIM = 128
FF = 768
TOPK = 8
EXP_DEV = 2
SLOTS_DEV = 3
PRE = 8
masked_score = -1e30
epsilon = 1e-06


def prefill_context(queries, new_keys, new_values):
    head_group = HEADS // KV_HEADS
    scaling = 1.0 / math.sqrt(HEAD_DIM)
    query_pre = queries[:PRE].reshape(PRE, KV_HEADS, head_group, HEAD_DIM)
    keys_pre = new_keys[:PRE].reshape(PRE, KV_HEADS, HEAD_DIM)
    values_pre = new_values[:PRE].reshape(PRE, KV_HEADS, HEAD_DIM)
    scores = (
        jnp.einsum("ikgd,jkd->kgij", query_pre, keys_pre, preferred_element_type=jnp.float32)
        * scaling
    )
    causal = jnp.arange(PRE)[:, None] >= jnp.arange(PRE)[None, :]
    scores = jnp.where(causal, scores, masked_score)
    exponent = jnp.exp(scores - jnp.max(scores, axis=-1, keepdims=True))
    attn_probs = (exponent / jnp.sum(exponent, axis=-1, keepdims=True)).astype(jnp.bfloat16)
    mixed_values = jnp.einsum(
        "kgij,jkd->ikgd", attn_probs, values_pre, preferred_element_type=jnp.float32
    )
    return mixed_values.astype(jnp.bfloat16).reshape(PRE, HEADS * HEAD_DIM)


def decode_context(queries, new_keys, new_values, key_cache, value_cache, cache_len):
    requests = key_cache.shape[0]
    cache_slots = key_cache.shape[1]
    head_group = HEADS // KV_HEADS
    scaling = 1.0 / math.sqrt(HEAD_DIM)
    query_dec = queries[PRE:].reshape(requests, KV_HEADS, head_group, HEAD_DIM)
    keys_dec = new_keys[PRE:].reshape(requests, KV_HEADS, HEAD_DIM)
    values_dec = new_values[PRE:].reshape(requests, KV_HEADS, HEAD_DIM)
    cached_keys = key_cache.reshape(requests, cache_slots, KV_HEADS, HEAD_DIM)
    cached_values = value_cache.reshape(requests, cache_slots, KV_HEADS, HEAD_DIM)
    cache_scores = (
        jnp.einsum("nkgd,ntkd->nkgt", query_dec, cached_keys, preferred_element_type=jnp.float32)
        * scaling
    )
    own_score = (
        jnp.einsum("nkgd,nkd->nkg", query_dec, keys_dec, preferred_element_type=jnp.float32)
        * scaling
    )
    valid = jnp.arange(cache_slots)[None, :] < cache_len[:, None]
    cache_scores = jnp.where(valid[:, None, None, :], cache_scores, masked_score)
    top_score = jnp.maximum(jnp.max(cache_scores, axis=-1), own_score)
    cache_exp = jnp.exp(cache_scores - top_score[..., None])
    own_exp = jnp.exp(own_score - top_score)
    denominator = jnp.sum(cache_exp, axis=-1) + own_exp
    cache_probs = (cache_exp / denominator[..., None]).astype(jnp.bfloat16)
    own_probs = (own_exp / denominator).astype(jnp.bfloat16)
    mixed_values = jnp.einsum(
        "nkgt,ntkd->nkgd", cache_probs, cached_values, preferred_element_type=jnp.float32
    )
    mixed_values = (
        mixed_values
        + own_probs.astype(jnp.float32)[..., None] * values_dec.astype(jnp.float32)[:, :, None, :]
    )
    return mixed_values.astype(jnp.bfloat16).reshape(requests, HEADS * HEAD_DIM)


def activate(summed):
    return (jax.nn.silu(summed[..., :FF]) * summed[..., FF:]).astype(jnp.bfloat16)


def local(
    queries,
    new_keys,
    new_values,
    key_cache,
    value_cache,
    cache_len,
    residual,
    out_proj,
    norm_gain,
    expert_ids,
    route_weights,
    slot_expert,
    gate_up,
    down_proj,
):
    rows_dev = queries.shape[0]
    width_part = out_proj.shape[1]
    ep_devices = lax.axis_size("ep")
    group_devices = lax.axis_size("grp")
    experts_all = EXP_DEV * ep_devices
    most_rows = min(rows_dev, (TOPK * rows_dev + experts_all - 2) // (experts_all - 1) + 1)
    context = jnp.concatenate(
        [
            prefill_context(queries, new_keys, new_values),
            decode_context(queries, new_keys, new_values, key_cache, value_cache, cache_len),
        ],
        axis=0,
    )
    context_col, ids_col, weights_col = (
        lax.all_gather(context, "grp", axis=0, tiled=True),
        lax.all_gather(expert_ids, "grp", axis=0, tiled=True),
        lax.all_gather(route_weights, "grp", axis=0, tiled=True),
    )
    residual_col = lax.all_to_all(residual, "grp", split_axis=1, concat_axis=0, tiled=True)
    attended = (
        residual_col.astype(jnp.float32)
        + jnp.dot(context_col, out_proj, preferred_element_type=jnp.float32)
    ).astype(jnp.bfloat16)
    attended_f = attended.astype(jnp.float32)
    sum_squares = lax.psum(jnp.sum(attended_f * attended_f, axis=1), "grp")
    normed = (
        attended_f * lax.rsqrt(sum_squares / D + epsilon)[:, None] * norm_gain[None, :]
    ).astype(jnp.bfloat16)
    route_share = weights_col.astype(jnp.float32)
    route_share = route_share / jnp.sum(route_share, axis=-1, keepdims=True)
    column_rows = normed.shape[0]
    slot_rows = 2 * group_devices
    ep_index = lax.axis_index("ep")
    ids_all = lax.all_gather(ids_col, "ep", axis=0)
    share_all = lax.all_gather(route_share, "ep", axis=0)
    rows_all = lax.all_gather(normed, "ep", axis=0)
    mine = lax.dynamic_slice_in_dim(slot_expert, ep_index * SLOTS_DEV, SLOTS_DEV)
    slots = jnp.arange(slot_expert.shape[0], dtype=jnp.int32)
    same = slot_expert[None, :] == mine[:, None]
    copies = jnp.sum(same, axis=1)
    place = ep_index * SLOTS_DEV + jnp.arange(SLOTS_DEV)
    copy_index = jnp.sum(same & (slots[None, :] < place[:, None]), axis=1)
    hit = ids_all[:, None, :, :] == mine[None, :, None, None]
    share = jnp.sum(jnp.where(hit, share_all[:, None, :, :], 0.0), axis=-1)
    named = jnp.any(hit, axis=-1)
    count = named.astype(jnp.int32)
    ranking = jnp.cumsum(count, axis=-1) - count
    position = ranking // copies[None, :, None]
    taken = named & (ranking % copies[None, :, None] == copy_index[None, :, None])
    pick = taken[:, :, None, :] & (
        position[:, :, None, :] == jnp.arange(slot_rows)[None, None, :, None]
    )
    received = jnp.einsum(
        "sjtr,srd->jstd", pick.astype(jnp.bfloat16), rows_all, preferred_element_type=jnp.float32
    ).astype(jnp.bfloat16)
    received = received.reshape(SLOTS_DEV, ep_devices * slot_rows, width_part)
    partial_term = jnp.einsum(
        "jnd,jdf->jnf", received, gate_up, preferred_element_type=jnp.float32
    ).astype(jnp.bfloat16)
    summed = lax.psum_scatter(partial_term, "grp", scatter_dimension=1, tiled=True)
    hidden = activate(summed.astype(jnp.float32))
    hidden = lax.all_gather(hidden, "grp", axis=1, tiled=True)
    expert_out = jnp.einsum(
        "jnh,jhd->jnd", hidden, down_proj, preferred_element_type=jnp.float32
    ).astype(jnp.bfloat16)
    expert_out = expert_out.reshape(SLOTS_DEV, ep_devices, slot_rows, width_part)
    weighted = jnp.where(pick, share[:, :, None, :], 0.0).astype(jnp.bfloat16)
    mixture = jnp.einsum(
        "sjtr,jstd->srd", weighted, expert_out, preferred_element_type=jnp.float32
    ).astype(jnp.bfloat16)
    mixture = lax.psum_scatter(mixture, "ep", scatter_dimension=0, tiled=False)
    mixture = mixture.astype(jnp.float32)
    moe_col = mixture.astype(jnp.bfloat16)
    layer_col = (attended_f + mixture).astype(jnp.bfloat16)
    moe_out, layer_out = (
        lax.all_to_all(moe_col, "grp", split_axis=0, concat_axis=1, tiled=True),
        lax.all_to_all(layer_col, "grp", split_axis=0, concat_axis=1, tiled=True),
    )
    return (moe_out, layer_out)


def solution(mesh):
    placed = (
        P(("grp", "ep"), None),
        P(("grp", "ep"), None),
        P(("grp", "ep"), None),
        P(("grp", "ep"), None, None),
        P(("grp", "ep"), None, None),
        P(("grp", "ep")),
        P(("grp", "ep"), None),
        P(None, "grp"),
        P("grp"),
        P(("grp", "ep"), None),
        P(("grp", "ep"), None),
        P(),
        P("ep", "grp", None),
        P("ep", None, "grp"),
    )
    return jax.shard_map(
        local,
        mesh=mesh,
        in_specs=placed,
        out_specs=(P(("grp", "ep"), None), P(("grp", "ep"), None)),
        check_vma=False,
    )
```

profile of v0, /device:TPU:2, one launch (start us, length us, event | category | flops | bytes accessed | tf_op | source)
XLA Modules:
  0.0 433.6 jit_solution(6127606662466355972)
XLA Ops:
  7.2 1.7 copy.121
  8.9 6.1 %all-to-all-start = ((bf16[24,4,512]{2,0,1:T(8,128)(2,1)}), bf16[24,4,512]{2,0,1:T(8,128)(2,1)}, u32[]{:S(2)}, u32[]{:S(2)}) async-start(bf16[24,4,512]{2,0,1:T(8,128)(2,1)} %bitcast.118), calls=%async_computation | async-start | bytes 196608 | tf_op jit(solution)/shard_map/all_to_all | solution.py:114
  17.4 1.3 iota_compare_fusion.1
  22.6 1.3 fusion.55
  24.8 13.3 %all_gather.36 = bf16[96,4096]{1,0:T(8,128)(2,1)S(1)} all-gather(bf16[24,4096]{1,0:T(8,128)(2,1)S(1)} %pad_maximum_fusion), channel_id=1, replica_groups=mesh['grp'=4,'ep'=64] {'grp'}, dimensions={0}, use_global_device_ids=true | all-gather | bytes 983040 | tf_op jit(solution)/shard_map/all_gather | solution.py:110
  39.0 3.1 multiply_reduce_fusion
  42.1 9.6 %psum.7 = f32[96]{0:T(128)S(1)} all-reduce(f32[96]{0:T(128)S(1)} %get-tuple-element.12), channel_id=1, replica_groups=mesh['grp'=4,'ep'=64] {'grp'}, use_global_device_ids=true, to_apply=%region_11.12 | all-reduce | flops 96 | bytes 768 | tf_op jit(solution)/shard_map/psum | solution.py:120
  52.6 10.7 %all-gather.3 = s32[4,24,8]{1,2,0:T(8,128)S(1)} all-gather(s32[1,24,8]{1,2,0:T(8,128)S(1)} %bitcast.133), channel_id=1, replica_groups=mesh['grp'=4,'ep'=64] {'grp'}, dimensions={0}, use_global_device_ids=true | all-gather | bytes 3840 | tf_op jit(solution)/shard_map/all_gather | solution.py:111
  63.5 46.5 %all-gather.4 = s32[64,96,8]{1,2,0:T(8,128)S(1)} all-gather(s32[1,96,8]{1,2,0:T(8,128)S(1)} %reshape.156), channel_id=2, replica_groups=mesh['grp'=4,'ep'=64] {'ep'}, dimensions={0}, use_global_device_ids=true | all-gather | bytes 199680 | tf_op jit(solution)/shard_map/all_gather | solution.py:129
  113.7 21.2 %all-gather.12.cloned.1.call-done = bf16[6144,512]{1,0:T(8,128)(2,1)} async-done(((bf16[96,512]{1,0:T(8,128)(2,1)}), bf16[6144,512]{1,0:T(8,128)(2,1)}) %all-gather.12.cloned.1.call-update) | async-done | bytes 6291472 | tf_op jit(solution)/shard_map/all_gather | solution.py:131
  134.9 3.7 fusion.5
  138.6 6.6 %convolution_convert_fusion = bf16[3,512,1536]{2,1,0:T(8,128)(2,1)} fusion(bf16[3,512,1536]{2,1,0:T(8,128)(2,1)} %param.26, bf16[3,64,8,512]{3,2,0,1:T(8,128)(2,1)S(1)} %fusion.5), kind=kOutput, calls=%fused_computation.2 | convolution fusion | flops 2418278400 | bytes 11010048 | tf_op jit(solution)/shard_map/jnd,jdf->jnf/dot_general | solution.py:152
  145.3 49.2 %reduce-scatter.3.cloned.1.call-done = bf16[3,128,1536]{2,1,0:T(8,128)(2,1)} async-done(((bf16[3,512,1536]{2,1,0:T(8,128)(2,1)}), bf16[3,128,1536]{2,1,0:T(8,128)(2,1)}) %reduce-scatter.3.cloned.1.call-update) | async-done | bytes 1179664 | tf_op jit(solution)/shard_map/reduce_scatter | solution.py:155
  194.5 1.5 convert_element_type.126
  197.3 10.2 %all-gather.5 = bf16[4,24,8]{1,2,0:T(8,128)(2,1)S(1)} all-gather(bf16[1,24,8]{1,2,0:T(8,128)(2,1)S(1)} %bitcast.134), channel_id=1, replica_groups=mesh['grp'=4,'ep'=64] {'grp'}, dimensions={0}, use_global_device_ids=true | all-gather | bytes 1920 | tf_op jit(solution)/shard_map/all_gather | solution.py:112
  207.7 45.3 %all-gather.6 = f32[64,96,8]{1,2,0:T(8,128)S(1)} all-gather(f32[1,96,8]{1,2,0:T(8,128)S(1)} %divide_bitcast_fusion), channel_id=3, replica_groups=mesh['grp'=4,'ep'=64] {'ep'}, dimensions={0}, use_global_device_ids=true | all-gather | bytes 199680 | tf_op jit(solution)/shard_map/all_gather | solution.py:130
  253.4 3.0 fusion.4
  256.5 4.5 %bitcast_convert_fusion = bf16[64,96,512]{2,1,0:T(8,128)(2,1)} fusion(bf16[3,64,8,512]{3,2,1,0:T(8,128)(2,1)S(1)} %fusion.4, bf16[64,3,96]{2,1,0:T(4,128)(2,1)S(1)} %fusion.15, s32[64,3,96]{2,1,0:T(4,128)S(1)} %copy.59, pred[64,3,96]{2,1,0:T(4,128)(4,1)S(1)} %copy.58), kind=kOutput, calls=%fused_computation.1 | convolution fusion | flops 154583040 | bytes 7993344 | tf_op jit(solution)/shard_map/sjtr,jstd->srd/dot_general | solution.py:163
  261.0 147.2 %reduce-scatter.5.cloned.1.call-done = bf16[1,96,512]{2,1,0:T(8,128)(2,1)} async-done(((bf16[64,96,512]{2,1,0:T(8,128)(2,1)}), bf16[1,96,512]{2,1,0:T(8,128)(2,1)}) %reduce-scatter.5.cloned.1.call-update) | async-done | bytes 98320 | tf_op jit(solution)/shard_map/reduce_scatter | solution.py:166
  408.1 4.8 %all-to-all-start.1 = ((bf16[4,24,512]{2,1,0:T(8,128)(2,1)}), bf16[4,24,512]{2,1,0:T(8,128)(2,1)S(1)}, u32[]{:S(2)}, u32[]{:S(2)}) async-start(bf16[4,24,512]{2,1,0:T(8,128)(2,1)} %bitcast.125), calls=%async_computation.3 | async-start | bytes 196608 | tf_op jit(solution)/shard_map/all_to_all | solution.py:171
  413.0 1.6 fusion.29
  414.6 2.8 all-to-all-done.1
  417.3 4.7 %all-to-all-start.2 = ((bf16[4,24,512]{2,1,0:T(8,128)(2,1)}), bf16[4,24,512]{2,1,0:T(8,128)(2,1)S(1)}, u32[]{:S(2)}, u32[]{:S(2)}) async-start(bf16[4,24,512]{2,1,0:T(8,128)(2,1)} %bitcast.27), calls=%async_computation.4 | async-start | bytes 196608 | tf_op jit(solution)/shard_map/all_to_all | solution.py:172
  422.7 3.7 all-to-all-done.2
  (69 shorter events, 15.8 us)
Async XLA Ops:
  7.2 246.2 %copy-start = (bf16[3,768,512]{2,1,0:T(8,128)(2,1)S(1)}, bf16[3,768,512]{2,1,0:T(8,128)(2,1)}, u32[]{:S(2)}) copy-start(bf16[3,768,512]{2,1,0:T(8,128)(2,1)} %param.27) | copy-start | bytes 7077892
  7.2 15.4 %copy-start.1 = (bf16[16,48,512]{2,1,0:T(8,128)(2,1)S(1)}, bf16[16,48,512]{2,1,0:T(8,128)(2,1)}, u32[]{:S(2)}) copy-start(bf16[16,48,512]{2,1,0:T(8,128)(2,1)} %param.17) | copy-start | bytes 2359300
  8.9 29.2 %all-to-all-start = ((bf16[24,4,512]{2,0,1:T(8,128)(2,1)}), bf16[24,4,512]{2,0,1:T(8,128)(2,1)}, u32[]{:S(2)}, u32[]{:S(2)}) async-start(bf16[24,4,512]{2,0,1:T(8,128)(2,1)} %bitcast.118), calls=%async_computation | async-start | bytes 196608 | tf_op jit(solution)/shard_map/all_to_all | solution.py:114
  15.0 119.9 %all-gather.12.cloned.1.call-start = ((), (), s32[]{:S(2)}) async-start(), calls=%async_computation.8 | async-start | bytes 6389760 | tf_op jit(solution)/shard_map/all_gather | solution.py:131
  21.5 2.8 copy-start.6
  39.0 12.8 %copy-start.3 = (f32[512]{0:T(512)S(1)}, f32[512]{0:T(512)}, u32[]{:S(2)}) copy-start(f32[512]{0:T(512)} %param.22) | copy-start | bytes 6148
  39.0 13.6 %copy-start.2 = (s32[24,8]{0,1:T(8,128)S(1)}, s32[24,8]{0,1:T(8,128)}, u32[]{:S(2)}) copy-start(s32[24,8]{0,1:T(8,128)} %param.23) | copy-start | bytes 2308
  39.0 24.4 %copy-start.5 = (s32[192]{0:T(256)S(1)}, s32[192]{0:T(256)}, u32[]{:S(2)}) copy-start(s32[192]{0:T(256)} %param.25) | copy-start | bytes 2308
  52.5 142.0 %reduce-scatter.3.cloned.1.call-start = ((), (), s32[]{:S(2)}) async-start(), calls=%async_computation.5 | async-start | bytes 5898240 | tf_op jit(solution)/shard_map/reduce_scatter | solution.py:155
  145.3 108.1 %all-gather.10.cloned.1.call-start = ((), (), s32[]{:S(2)}) async-start(), calls=%async_computation.6 | async-start | bytes 2949120 | tf_op jit(solution)/shard_map/all_gather | solution.py:157
  196.0 1.3 copy-start.4
  197.3 210.9 %reduce-scatter.5.cloned.1.call-start = ((), (), s32[]{:S(2)}) async-start(), calls=%async_computation.7 | async-start | bytes 6389760 | tf_op jit(solution)/shard_map/reduce_scatter | solution.py:166
  408.1 9.2 %all-to-all-start.1 = ((bf16[4,24,512]{2,1,0:T(8,128)(2,1)}), bf16[4,24,512]{2,1,0:T(8,128)(2,1)S(1)}, u32[]{:S(2)}, u32[]{:S(2)}) async-start(bf16[4,24,512]{2,1,0:T(8,128)(2,1)} %bitcast.125), calls=%async_computation.3 | async-start | bytes 196608 | tf_op jit(solution)/shard_map/all_to_all | solution.py:171
  417.3 9.1 %all-to-all-start.2 = ((bf16[4,24,512]{2,1,0:T(8,128)(2,1)}), bf16[4,24,512]{2,1,0:T(8,128)(2,1)S(1)}, u32[]{:S(2)}, u32[]{:S(2)}) async-start(bf16[4,24,512]{2,1,0:T(8,128)(2,1)} %bitcast.27), calls=%async_computation.4 | async-start | bytes 196608 | tf_op jit(solution)/shard_map/all_to_all | solution.py:172
Sparse Core Ops, SparseCore 0:
  52.6 82.2 all-gather.11
  145.4 49.0 reduce-scatter.2
  197.4 35.6 all-gather.9
  261.1 147.0 reduce-scatter.4
where the time goes:
time: 435 us; the launch traced here: 434 us
  waiting for transfers between devices  224 us (51%)
  blocking collectives  136 us (31%)
  matrix products  24.9 us (6%)
  starting transfers between devices  15.8 us (4%)
  between operations  14 us (3%)
  other arithmetic  12.9 us (3%)
  local copies, waits for them, and re-layouts  6.18 us (1%)
    reduce_scatter x1, waiting for transfers between devices, local(): mixture = lax.psum_scatter(mixture, 'ep', scatter_dimension=0, tiled=False)  147 us
    reduce_scatter x1, waiting for transfers between devices, local(): lax.psum_scatter(partial_term, 'grp', scatter_dimension=1, tiled=True)  49.2 us
    all_gather x1, blocking collectives, local(): ids_all = lax.all_gather(ids_col, 'ep', axis=0)  46.5 us
    all_gather x1, blocking collectives, local(): share_all = lax.all_gather(route_share, 'ep', axis=0)  45.3 us
    all_gather x1, waiting for transfers between devices, local(): rows_all = lax.all_gather(normed, 'ep', axis=0)  21.2 us
    all_gather x1, blocking collectives, local(): lax.all_gather(context, 'grp', axis=0, tiled=True)  13.3 us
    all_gather x1, blocking collectives, local(): lax.all_gather(expert_ids, 'grp', axis=0, tiled=True)  10.7 us
    all_gather x1, blocking collectives, local(): lax.all_gather(route_weights, 'grp', axis=0, tiled=True)  10.2 us
  transfers between devices with their start and end apart: 7, of which 5 were waited for; matrix products, arithmetic and copies ran while one was open for 4% of the time, Pallas kernels for 0%

commit v1 on v0

--- a/solution.py
+++ b/solution.py
@@ -108,7 +108,9 @@
     )
     context_col, ids_col, weights_col = (
         lax.all_gather(context, "grp", axis=0, tiled=True),
-        lax.all_gather(expert_ids, "grp", axis=0, tiled=True),
+        jnp.concatenate(
+            lax.all_to_all(jnp.stack([expert_ids] * lax.axis_size("grp")), "grp", 0, 0), axis=0
+        ),
         lax.all_gather(route_weights, "grp", axis=0, tiled=True),
     )
     residual_col = lax.all_to_all(residual, "grp", split_axis=1, concat_axis=0, tiled=True)

time: 435 us -> 434 us (level)
  blocking collectives: 136 us -> 126 us
  starting transfers between devices: 15.8 us -> 20.3 us
    all_gather x1 -> x0, blocking collectives: 10.7 us -> none  [local(): lax.all_gather(expert_ids, 'grp', axis=0, tiled=True)]
    all_to_all x0 -> x1, starting transfers between devices: none -> 4.56 us  [local(): lax.all_to_all(jnp.stack([expert_ids] * lax.axis_size('grp')), 'grp', 0, 0)]
  transfers between devices with their start and end apart: 7 -> 8, of which waited for: 5 -> 6; matrix products, arithmetic and copies ran while one was open for 4% -> 4% of each run, Pallas kernels for 0% -> 0%
where the time goes in v1:
time: 434 us; the launch traced here: 433 us
  waiting for transfers between devices  227 us (52%)
  blocking collectives  126 us (29%)
  matrix products  24.9 us (6%)
  starting transfers between devices  20.3 us (5%)
  between operations  14 us (3%)
  other arithmetic  13.6 us (3%)
  local copies, waits for them, and re-layouts  7.44 us (2%)
    reduce_scatter x1, waiting for transfers between devices, local(): mixture = lax.psum_scatter(mixture, 'ep', scatter_dimension=0, tiled=False)  147 us
    reduce_scatter x1, waiting for transfers between devices, local(): lax.psum_scatter(partial_term, 'grp', scatter_dimension=1, tiled=True)  49.2 us
    all_gather x1, blocking collectives, local(): ids_all = lax.all_gather(ids_col, 'ep', axis=0)  47.2 us
    all_gather x1, blocking collectives, local(): share_all = lax.all_gather(route_share, 'ep', axis=0)  45.2 us
    all_gather x1, waiting for transfers between devices, local(): rows_all = lax.all_gather(normed, 'ep', axis=0)  21.3 us
    all_gather x1, blocking collectives, local(): lax.all_gather(context, 'grp', axis=0, tiled=True)  13.3 us
    all_gather x1, blocking collectives, local(): lax.all_gather(route_weights, 'grp', axis=0, tiled=True)  10.2 us
    psum x1, blocking collectives, local(): sum_squares = lax.psum(jnp.sum(attended_f * attended_f, axis=1), 'grp')  9.61 us
  transfers between devices with their start and end apart: 8, of which 6 were waited for; matrix products, arithmetic and copies ran while one was open for 4% of the time, Pallas kernels for 0%

profile of v1, /device:TPU:2, one launch (start us, length us, event | category | flops | bytes accessed | tf_op | source)
XLA Modules:
  0.0 433.2 jit_solution(17004051154045625159)
XLA Ops:
  7.2 1.7 copy.135
  8.9 6.1 %all-to-all-start.1 = ((bf16[24,4,512]{2,0,1:T(8,128)(2,1)}), bf16[24,4,512]{2,0,1:T(8,128)(2,1)}, u32[]{:S(2)}, u32[]{:S(2)}) async-start(bf16[24,4,512]{2,0,1:T(8,128)(2,1)} %bitcast.120), calls=%async_computation.1 | async-start | bytes 196608 | tf_op jit(solution)/shard_map/all_to_all | solution.py:116
  17.4 1.3 iota_compare_fusion.1
  24.8 13.3 %all_gather.28 = bf16[96,4096]{1,0:T(8,128)(2,1)S(1)} all-gather(bf16[24,4096]{1,0:T(8,128)(2,1)S(1)} %pad_maximum_fusion), channel_id=1, replica_groups=mesh['grp'=4,'ep'=64] {'grp'}, dimensions={0}, use_global_device_ids=true | all-gather | bytes 983040 | tf_op jit(solution)/shard_map/all_gather | solution.py:110
  39.0 3.1 multiply_reduce_fusion
  42.1 9.6 %psum.7 = f32[96]{0:T(128)S(1)} all-reduce(f32[96]{0:T(128)S(1)} %get-tuple-element.12), channel_id=1, replica_groups=mesh['grp'=4,'ep'=64] {'grp'}, use_global_device_ids=true, to_apply=%region_11.12 | all-reduce | flops 96 | bytes 768 | tf_op jit(solution)/shard_map/psum | solution.py:122
  53.2 4.6 %all-to-all-start = ((s32[4,1,192]{2,1,0:T(1,128)}), s32[4,1,192]{2,1,0:T(1,128)S(1)}, u32[]{:S(2)}, u32[]{:S(2)}) async-start(s32[4,1,192]{2,1,0:T(1,128)} %reshape.170), calls=%async_computation | async-start | bytes 8192 | tf_op jit(solution)/shard_map/all_to_all | solution.py:112
  58.1 3.5 all-to-all-done
  63.0 47.2 %all_gather.24 = s32[64,96,8]{1,2,0:T(8,128)S(1)} all-gather(s32[1,96,8]{1,2,0:T(8,128)S(1)} %all_gather_reshape.3), channel_id=1, replica_groups=mesh['grp'=4,'ep'=64] {'ep'}, dimensions={0}, use_global_device_ids=true | all-gather | bytes 199680 | tf_op jit(solution)/shard_map/all_gather | solution.py:131
  113.6 21.3 %all-gather.9.cloned.1.call-done = bf16[6144,512]{1,0:T(8,128)(2,1)} async-done(((bf16[96,512]{1,0:T(8,128)(2,1)}), bf16[6144,512]{1,0:T(8,128)(2,1)}) %all-gather.9.cloned.1.call-update) | async-done | bytes 6291472 | tf_op jit(solution)/shard_map/all_gather | solution.py:133
  134.9 3.7 fusion.5
  138.6 6.6 %convolution_convert_fusion = bf16[3,512,1536]{2,1,0:T(8,128)(2,1)} fusion(bf16[3,512,1536]{2,1,0:T(8,128)(2,1)} %param.26, bf16[3,64,8,512]{3,2,0,1:T(8,128)(2,1)S(1)} %fusion.5), kind=kOutput, calls=%fused_computation.2 | convolution fusion | flops 2418278400 | bytes 11010048 | tf_op jit(solution)/shard_map/jnd,jdf->jnf/dot_general | solution.py:154
  145.3 49.2 %reduce-scatter.3.cloned.1.call-done = bf16[3,128,1536]{2,1,0:T(8,128)(2,1)} async-done(((bf16[3,512,1536]{2,1,0:T(8,128)(2,1)}), bf16[3,128,1536]{2,1,0:T(8,128)(2,1)}) %reduce-scatter.3.cloned.1.call-update) | async-done | bytes 1179664 | tf_op jit(solution)/shard_map/reduce_scatter | solution.py:157
  194.5 1.5 convert_element_type.126
  197.3 10.2 %all-gather.2 = bf16[4,24,8]{1,2,0:T(8,128)(2,1)S(1)} all-gather(bf16[1,24,8]{1,2,0:T(8,128)(2,1)S(1)} %bitcast.136), channel_id=1, replica_groups=mesh['grp'=4,'ep'=64] {'grp'}, dimensions={0}, use_global_device_ids=true | all-gather | bytes 1920 | tf_op jit(solution)/shard_map/all_gather | solution.py:114
  207.7 45.2 %all-gather.3 = f32[64,96,8]{1,2,0:T(8,128)S(1)} all-gather(f32[1,96,8]{1,2,0:T(8,128)S(1)} %divide_bitcast_fusion), channel_id=2, replica_groups=mesh['grp'=4,'ep'=64] {'ep'}, dimensions={0}, use_global_device_ids=true | all-gather | bytes 199680 | tf_op jit(solution)/shard_map/all_gather | solution.py:132
  253.4 3.0 fusion.4
  256.5 4.5 %bitcast_convert_fusion = bf16[64,96,512]{2,1,0:T(8,128)(2,1)} fusion(bf16[3,64,8,512]{3,2,1,0:T(8,128)(2,1)S(1)} %fusion.4, bf16[64,3,96]{2,1,0:T(4,128)(2,1)S(1)} %fusion.15, s32[64,3,96]{2,1,0:T(4,128)S(1)} %copy.73, pred[64,3,96]{2,1,0:T(4,128)(4,1)S(1)} %copy.72), kind=kOutput, calls=%fused_computation.1 | convolution fusion | flops 154583040 | bytes 7993344 | tf_op jit(solution)/shard_map/sjtr,jstd->srd/dot_general | solution.py:165
  261.0 146.9 %reduce-scatter.5.cloned.1.call-done = bf16[1,96,512]{2,1,0:T(8,128)(2,1)} async-done(((bf16[64,96,512]{2,1,0:T(8,128)(2,1)}), bf16[1,96,512]{2,1,0:T(8,128)(2,1)}) %reduce-scatter.5.cloned.1.call-update) | async-done | bytes 98320 | tf_op jit(solution)/shard_map/reduce_scatter | solution.py:168
  407.9 4.7 %all-to-all-start.2 = ((bf16[4,24,512]{2,1,0:T(8,128)(2,1)}), bf16[4,24,512]{2,1,0:T(8,128)(2,1)S(1)}, u32[]{:S(2)}, u32[]{:S(2)}) async-start(bf16[4,24,512]{2,1,0:T(8,128)(2,1)} %bitcast.127), calls=%async_computation.4 | async-start | bytes 196608 | tf_op jit(solution)/shard_map/all_to_all | solution.py:173
  412.6 1.6 fusion.29
  414.2 2.8 all-to-all-done.2
  416.9 4.7 %all-to-all-start.3 = ((bf16[4,24,512]{2,1,0:T(8,128)(2,1)}), bf16[4,24,512]{2,1,0:T(8,128)(2,1)S(1)}, u32[]{:S(2)}, u32[]{:S(2)}) async-start(bf16[4,24,512]{2,1,0:T(8,128)(2,1)} %bitcast.26), calls=%async_computation.5 | async-start | bytes 196608 | tf_op jit(solution)/shard_map/all_to_all | solution.py:174
  422.3 3.7 all-to-all-done.3
  (75 shorter events, 19.0 us)
Async XLA Ops:
  7.2 246.2 %copy-start = (bf16[3,768,512]{2,1,0:T(8,128)(2,1)S(1)}, bf16[3,768,512]{2,1,0:T(8,128)(2,1)}, u32[]{:S(2)}) copy-start(bf16[3,768,512]{2,1,0:T(8,128)(2,1)} %param.27) | copy-start | bytes 7077892
  7.2 15.4 %copy-start.1 = (bf16[16,48,512]{2,1,0:T(8,128)(2,1)S(1)}, bf16[16,48,512]{2,1,0:T(8,128)(2,1)}, u32[]{:S(2)}) copy-start(bf16[16,48,512]{2,1,0:T(8,128)(2,1)} %param.17) | copy-start | bytes 2359300
  8.9 29.2 %all-to-all-start.1 = ((bf16[24,4,512]{2,0,1:T(8,128)(2,1)}), bf16[24,4,512]{2,0,1:T(8,128)(2,1)}, u32[]{:S(2)}, u32[]{:S(2)}) async-start(bf16[24,4,512]{2,0,1:T(8,128)(2,1)} %bitcast.120), calls=%async_computation.1 | async-start | bytes 196608 | tf_op jit(solution)/shard_map/all_to_all | solution.py:116
  15.0 119.9 %all-gather.9.cloned.1.call-start = ((), (), s32[]{:S(2)}) async-start(), calls=%async_computation.9 | async-start | bytes 6389760 | tf_op jit(solution)/shard_map/all_gather | solution.py:133
  21.5 2.8 copy-start.6
  39.0 12.8 %copy-start.3 = (f32[512]{0:T(512)S(1)}, f32[512]{0:T(512)}, u32[]{:S(2)}) copy-start(f32[512]{0:T(512)} %param.22) | copy-start | bytes 6148
  39.0 13.5 %copy-start.2 = (s32[24,8]{0,1:T(8,128)S(1)}, s32[24,8]{0,1:T(8,128)}, u32[]{:S(2)}) copy-start(s32[24,8]{0,1:T(8,128)} %param.23) | copy-start | bytes 2308
  39.0 18.8 %copy-start.5 = (s32[192]{0:T(256)S(1)}, s32[192]{0:T(256)}, u32[]{:S(2)}) copy-start(s32[192]{0:T(256)} %param.25) | copy-start | bytes 2308
  53.2 8.4 %all-to-all-start = ((s32[4,1,192]{2,1,0:T(1,128)}), s32[4,1,192]{2,1,0:T(1,128)S(1)}, u32[]{:S(2)}, u32[]{:S(2)}) async-start(s32[4,1,192]{2,1,0:T(1,128)} %reshape.170), calls=%async_computation | async-start | bytes 8192 | tf_op jit(solution)/shard_map/all_to_all | solution.py:112
  57.8 136.7 %reduce-scatter.3.cloned.1.call-start = ((), (), s32[]{:S(2)}) async-start(), calls=%async_computation.6 | async-start | bytes 5898240 | tf_op jit(solution)/shard_map/reduce_scatter | solution.py:157
  145.3 108.1 %all-gather.7.cloned.1.call-start = ((), (), s32[]{:S(2)}) async-start(), calls=%async_computation.7 | async-start | bytes 2949120 | tf_op jit(solution)/shard_map/all_gather | solution.py:159
  196.0 1.3 copy-start.4
  197.3 210.6 %reduce-scatter.5.cloned.1.call-start = ((), (), s32[]{:S(2)}) async-start(), calls=%async_computation.8 | async-start | bytes 6389760 | tf_op jit(solution)/shard_map/reduce_scatter | solution.py:168
  407.9 9.1 %all-to-all-start.2 = ((bf16[4,24,512]{2,1,0:T(8,128)(2,1)}), bf16[4,24,512]{2,1,0:T(8,128)(2,1)S(1)}, u32[]{:S(2)}, u32[]{:S(2)}) async-start(bf16[4,24,512]{2,1,0:T(8,128)(2,1)} %bitcast.127), calls=%async_computation.4 | async-start | bytes 196608 | tf_op jit(solution)/shard_map/all_to_all | solution.py:173
  416.9 9.1 %all-to-all-start.3 = ((bf16[4,24,512]{2,1,0:T(8,128)(2,1)}), bf16[4,24,512]{2,1,0:T(8,128)(2,1)S(1)}, u32[]{:S(2)}, u32[]{:S(2)}) async-start(bf16[4,24,512]{2,1,0:T(8,128)(2,1)} %bitcast.26), calls=%async_computation.5 | async-start | bytes 196608 | tf_op jit(solution)/shard_map/all_to_all | solution.py:174
Sparse Core Ops, SparseCore 0:
  52.6 82.2 all-gather.8
  145.4 49.0 reduce-scatter.2
  197.4 35.6 all-gather.6
  261.1 146.7 reduce-scatter.4
